TPU v7x, 512 devices: a whole 4x4x16 slice. The times are simulated.
512 devices in a mesh: dp: 32 (over z_lo, x), mp: 16 (over z_hi, y, core).
Axes of the slice: x: 4, y: 4, z: 16 (z_hi: 2, z_lo: 8; z = z_hi * 8 + z_lo), core: 2. Of those that a mesh axis runs over, the one named last changes fastest.
Arguments:
- x_tiles: bfloat16 [32768, 6144], P('dp', 'mp')
- counts: int32 [32, 32], replicated, may hold values from 4 to 28, as said below
- owners: int32 [32, 32], replicated, may hold values from 0 to 31, as said below
- ln_gain: bfloat16 [6144], P('mp'), may hold values from 0.5 to 1.5
- w_up: bfloat16 [6144, 12288], P('dp', 'mp'), may hold values from -0.078125 to 0.078125
- up_bias: bfloat16 [12288], P('mp'), may hold values from -3 to 3
Outputs:
- hidden_act: bfloat16 [16384, 12288], P('dp', 'mp')
Inputs may be any that keep to these rules, and one draw needn't show every extreme that they name: Each row of owners is a permutation of 0 .. 31. Tile t of group s holds counts[s, t] patches in its first slots; every group takes exactly 512 patches in all.
All inputs are finite; a program needn't handle non-finite values.
Results may differ from a plain program's by a relative error of at most 0.0047.
Values may be sent and summed in bfloat16 or wider, within the bound.
No kernel may reach another device: no remote copies, remote signals or barrier semaphores. Data moves between devices by JAX's collectives and lax.ppermute only.
A program may use at most 64 MiB of HBM per device.

v0:
```python
import jax
import jax.numpy as jnp
from jax import lax
from jax.sharding import PartitionSpec as P

D = 6144
RECV = 512


def local(x_tiles, counts, owners, ln_gain, w_up, up_bias):
    groups = lax.axis_size("dp")
    my_index = lax.axis_index("dp")
    tile_rows = x_tiles.shape[0] // groups
    width_part = x_tiles.shape[1]
    tile_block = x_tiles.reshape(groups, tile_rows, width_part)
    inverse = jnp.argsort(owners, axis=1)
    my_tiles = lax.dynamic_index_in_dim(inverse, my_index, 0, keepdims=False)
    outgoing = jnp.take(tile_block, my_tiles, axis=0)
    incoming = lax.all_to_all(outgoing, "dp", split_axis=0, concat_axis=0, tiled=True)
    slot_count = incoming.shape[1]
    source_tiles = lax.dynamic_index_in_dim(inverse, my_index, 1, keepdims=False)
    held_rows = jnp.take_along_axis(counts, source_tiles[:, None], axis=1)[:, 0]
    inclusive = jnp.cumsum(held_rows)
    exclusive = inclusive - held_rows
    positions = jnp.arange(RECV, dtype=jnp.int32)
    source = jnp.sum((inclusive[None, :] <= positions[:, None]).astype(jnp.int32), axis=1)
    slot_index = positions - jnp.take(exclusive, source)
    flat_index = source * slot_count + slot_index
    packed = jnp.take(incoming.reshape(groups * slot_count, width_part), flat_index, axis=0)
    as_float = packed.astype(jnp.float32)
    row_sum, row_square = lax.psum(
        (jnp.sum(as_float, axis=1), jnp.sum(as_float * as_float, axis=1)), "mp"
    )
    row_mean = row_sum / D
    variance = row_square / D - row_mean * row_mean
    scaled = (
        (as_float - row_mean[:, None])
        * lax.rsqrt(variance + 1e-06)[:, None]
        * ln_gain.astype(jnp.float32)
    )
    normed = lax.all_gather(scaled.astype(jnp.bfloat16), "mp", axis=1, tiled=True)
    projected = jnp.dot(
        normed, lax.all_gather(w_up, "dp", axis=0, tiled=True), preferred_element_type=jnp.float32
    )
    return jax.nn.gelu(projected + up_bias.astype(jnp.float32), approximate=False).astype(
        jnp.bfloat16
    )


def solution(mesh):
    return jax.shard_map(
        local,
        mesh=mesh,
        in_specs=(P("dp", "mp"), P(), P(), P("mp"), P("dp", "mp"), P("mp")),
        out_specs=P("dp", "mp"),
        check_vma=False,
    )
```

profile of v0, /device:TPU:2, one launch (start us, length us, event | category | flops | bytes accessed | tf_op | source)
XLA Modules:
  0.0 536.9 jit_solution(3228038346032233318)
XLA Ops:
  6.5 0.0 copy-start
  6.5 0.9 copy.10
  7.4 0.8 sort.17
  8.2 0.2 dynamic-slice_reduce_fusion
  8.5 0.0 copy-done
  8.5 0.7 gather_fusion
  9.2 0.0 copy-start.3
  9.2 0.0 copy-start.1
  9.2 1.0 broadcast_select_fusion
  10.3 15.7 %all-to-all-start = ((bf16[32,32,384]{2,1,0:T(8,128)(2,1)}), bf16[32,32,384]{2,1,0:T(8,128)(2,1)S(1)}, u32[]{:S(2)}, u32[]{:S(2)}) async-start(bf16[32,32,384]{2,1,0:T(8,128)(2,1)} %broadcast_select_fusion), calls=%async_computation | async-start | bytes 1572864 | tf_op jit(solution)/shard_map/all_to_all | solution.py:19
  26.0 0.0 all-gather.3.cloned.1.call-start
  26.0 0.0 copy-done.3
  26.0 0.0 copy-done.1
  26.0 0.7 gather_fusion.2
  26.8 0.1 copy.11
  26.9 0.1 reduce-window.8
  26.9 0.1 reduce
  27.0 0.7 fusion.18
  27.8 0.7 fusion.17
  28.5 0.1 convert_reduce_fusion.1
  28.6 4.4 compare_select_fusion.2
  33.0 0.2 compare_reduce_fusion.24
  33.1 15.7 %compare_and_fusion.1 = (pred[512]{0:T(512)(128)(4,1)S(1)}, s32[512]{0:T(512)S(1)}) fusion(s32[512]{0:T(512)S(1)} %convert_reduce_fusion.1, pred[512]{0:T(512)(128)(4,1)S(1)} %get-tuple-element.33, pred[512]{0:T(512)(128)(4,1)S(1)} %get-tuple-element.31, pred[512]{0:T(512)(128)(4,1)S(1)} %get-tuple-element.32, pred[512]{0:T(512)(128)(4,1)S(1)} %get-tuple-element.30, ...), kind=kLoop, calls=%fused_computation.79 | loop fusion | flops 20992 | bytes 19556 | tf_op jit(solution)/shard_map/jit(_take)/and | solution.py:29
  48.8 16.4 %all-to-all-done = bf16[32,32,384]{2,1,0:T(8,128)(2,1)S(1)} async-done(((bf16[32,32,384]{2,1,0:T(8,128)(2,1)}), bf16[32,32,384]{2,1,0:T(8,128)(2,1)S(1)}, u32[]{:S(2)}, u32[]{:S(2)}) %all-to-all-start) | async-done | bytes 786464 | tf_op jit(solution)/shard_map/all_to_all | solution.py:19
  65.3 1.9 gather_fusion.1
  67.2 0.0 copy-start.2
  67.2 0.4 convert_reduce_fusion
  67.6 67.1 %all-reduce = (f32[512]{0:T(512)S(1)}, f32[512]{0:T(512)S(1)}) all-reduce(f32[512]{0:T(512)S(1)} %get-tuple-element.8, f32[512]{0:T(512)S(1)} %get-tuple-element.7), channel_id=1, replica_groups=mesh['dp'=32,'mp'=16] {'mp'}, use_global_device_ids=true, to_apply=%region_6.7 | all-reduce | flops 1024 | bytes 8192 | tf_op jit(solution)/shard_map/psum | solution.py:31
  134.7 1.0 fusion.12
  135.7 0.0 all-gather.3.cloned.1.call-update
  135.8 0.0 all-gather.5.cloned.1.call-start
  135.8 0.7 all-gather.5.cloned.1.call-update
  136.5 0.0 copy-done.2
  136.5 140.3 %all-gather.3.cloned.1.call-done = bf16[512,6144]{1,0:T(8,128)(2,1)} async-done(((bf16[512,384]{1,0:T(8,128)(2,1)}), bf16[512,6144]{1,0:T(8,128)(2,1)}) %all-gather.3.cloned.1.call-update) | async-done | bytes 6291472 | tf_op jit(solution)/shard_map/all_gather | solution.py:41
  276.8 239.5 %all-gather.5.cloned.1.call-done = bf16[6144,768]{1,0:T(8,128)(2,1)} async-done(((bf16[192,768]{1,0:T(8,128)(2,1)}), bf16[6144,768]{1,0:T(8,128)(2,1)}) %all-gather.5.cloned.1.call-update) | async-done | bytes 9437200 | tf_op jit(solution)/shard_map/all_gather | solution.py:43
  516.4 13.7 %fusion.2 = bf16[512,768]{1,0:T(8,128)(2,1)} fusion(bf16[512,6144]{1,0:T(8,128)(2,1)} %all-gather.3.cloned.1.call-done, bf16[6144,768]{1,0:T(8,128)(2,1)} %all-gather.5.cloned.1.call-done, f32[768]{0:T(1024)S(1)} %convert_element_type.22), kind=kOutput, calls=%fused_computation.6 | convolution fusion | flops 4857790464 | bytes 16518144 | tf_op jit(solution)/shard_map/dot_general | solution.py:42
  (14 shorter events, 0.1 us)
Async XLA Ops:
  6.5 1.9 copy-start
  9.2 16.8 %copy-start.3 = (bf16[384]{0:T(512)(128)(2,1)S(1)}, bf16[384]{0:T(512)(128)(2,1)}, u32[]{:S(2)}) copy-start(bf16[384]{0:T(512)(128)(2,1)} %param.9) | copy-start | bytes 2308
  9.2 16.8 %copy-start.1 = (s32[32,32]{1,0:T(8,128)S(1)}, s32[32,32]{1,0:T(8,128)}, u32[]{:S(2)}) copy-start(s32[32,32]{1,0:T(8,128)} %param.7) | copy-start | bytes 12292
  10.3 55.0 %all-to-all-start = ((bf16[32,32,384]{2,1,0:T(8,128)(2,1)}), bf16[32,32,384]{2,1,0:T(8,128)(2,1)S(1)}, u32[]{:S(2)}, u32[]{:S(2)}) async-start(bf16[32,32,384]{2,1,0:T(8,128)(2,1)} %broadcast_select_fusion), calls=%async_computation | async-start | bytes 1572864 | tf_op jit(solution)/shard_map/all_to_all | solution.py:19
  26.0 250.9 %all-gather.3.cloned.1.call-start = ((), (), s32[]{:S(2)}) async-start(), calls=%async_computation.1 | async-start | bytes 6684672 | tf_op jit(solution)/shard_map/all_gather | solution.py:41
  67.2 69.3 %copy-start.2 = (bf16[768]{0:T(1024)(128)(2,1)S(1)}, bf16[768]{0:T(1024)(128)(2,1)}, u32[]{:S(2)}) copy-start(bf16[768]{0:T(1024)(128)(2,1)} %param.11) | copy-start | bytes 4612
  135.8 380.6 %all-gather.5.cloned.1.call-start = ((), (), s32[]{:S(2)}) async-start(), calls=%async_computation.2 | async-start | bytes 9732096 | tf_op jit(solution)/shard_map/all_gather | solution.py:43
Sparse Core Ops, SparseCore 0:
  135.9 140.8 all-gather.2
  278.9 237.4 all-gather.4
where the time goes:
time: 537 us
  waiting for transfers between devices  397 us (74%)
  blocking collectives  67.1 us (12%)
  other arithmetic  23.8 us (4%)
  starting transfers between devices  15.8 us (3%)
  matrix products  13.7 us (3%)
  between operations  13.6 us (3%)
  local copies, waits for them, and re-layouts  5.97 us (1%)
    all_gather x1, waiting for transfers between devices, local(): lax.all_gather(w_up, 'dp', axis=0, tiled=True)  240 us
    all_gather x1, waiting for transfers between devices, local(): lax.all_gather(scaled.astype(jnp.bfloat16), 'mp', axis=1, tiled=True)  140 us
    psum x1, blocking collectives, local(): lax.psum((jnp.sum(as_float, axis=1), jnp.sum(as_float * as_float, axis=1)...  67.1 us
    all_to_all x1, waiting for transfers between devices, local(): lax.all_to_all(outgoing, 'dp', split_axis=0, concat_axis=0, tiled=True)  16.4 us
    and x1, other arithmetic, local(): jnp.take(incoming.reshape(groups * slot_count, width_part), flat_index, a...  15.7 us
    all_to_all x1, starting transfers between devices, local(): lax.all_to_all(outgoing, 'dp', split_axis=0, concat_axis=0, tiled=True)  15.7 us
    dot_general x1, matrix products, local(): jnp.dot(normed, lax.all_gather(w_up, 'dp', axis=0, tiled=True), preferred...  13.7 us
  transfers between devices with their start and end apart: 3, of which 3 were waited for; matrix products, arithmetic and copies ran while one was open for 4% of the time, Pallas kernels for 0%

commit v1 on v0

--- a/solution.py
+++ b/solution.py
@@ -1,3 +1,4 @@
+import functools
 import jax
 import jax.numpy as jnp
 from jax import lax
@@ -5,6 +6,15 @@
 
 D = 6144
 RECV = 512
+
+
+def _define_packet(buf, peer_axis):
+    return jnp.concatenate(
+        lax.all_to_all(jnp.stack([buf] * lax.axis_size(peer_axis)), peer_axis, 0, 0), axis=1
+    )
+
+
+_manage_wires = functools.partial(_define_packet, peer_axis="mp")
 
 
 def local(x_tiles, counts, owners, ln_gain, w_up, up_bias):
@@ -38,7 +48,7 @@
         * lax.rsqrt(variance + 1e-06)[:, None]
         * ln_gain.astype(jnp.float32)
     )
-    normed = lax.all_gather(scaled.astype(jnp.bfloat16), "mp", axis=1, tiled=True)
+    normed = _manage_wires(scaled.astype(jnp.bfloat16))
     projected = jnp.dot(
         normed, lax.all_gather(w_up, "dp", axis=0, tiled=True), preferred_element_type=jnp.float32
     )

time: 537 us -> 624 us (1.16)
  the two profiles are of different devices: /device:TPU:2 before, /device:TPU:264 now
where the time goes in v1:
time: 624 us; the launch traced here: 623 us
  waiting for transfers between devices  478 us (77%)
  blocking collectives  52.2 us (8%)
  starting transfers between devices  32.6 us (5%)
  other arithmetic  23.1 us (4%)
  matrix products  13.8 us (2%)
  between operations  13.6 us (2%)
  local copies, waits for them, and re-layouts  9.39 us (2%)
    all_gather x1, waiting for transfers between devices, local(): lax.all_gather(w_up, 'dp', axis=0, tiled=True)  460 us
    psum x1, blocking collectives, local(): lax.psum((jnp.sum(as_float, axis=1), jnp.sum(as_float * as_float, axis=1)...  52.2 us
    all_to_all x1, starting transfers between devices, _define_packet(): lax.all_to_all(jnp.stack([buf] * lax.axis_size(peer_axis)), peer_axis, 0, 0)  24.7 us
    all_to_all x1, waiting for transfers between devices, local(): lax.all_to_all(outgoing, 'dp', split_axis=0, concat_axis=0, tiled=True)  18.1 us
    and x1, other arithmetic, local(): jnp.take(incoming.reshape(groups * slot_count, width_part), flat_index, a...  15.7 us
    dot_general x1, matrix products, local(): jnp.dot(normed, lax.all_gather(w_up, 'dp', axis=0, tiled=True), preferred...  13.8 us
  transfers between devices with their start and end apart: 3, of which 2 were waited for; matrix products, arithmetic and copies ran while one was open for 4% of the time, Pallas kernels for 0%

profile of v1, /device:TPU:264, one launch (start us, length us, event | category | flops | bytes accessed | tf_op | source)
XLA Modules:
  0.0 623.1 jit_solution(15422080609335362725)
XLA Ops:
  6.5 0.0 copy-start
  6.5 0.9 copy.11
  7.4 0.8 sort.17
  8.2 0.2 dynamic-slice_reduce_fusion
  8.5 0.0 copy-done
  8.5 0.7 gather_fusion
  9.2 0.0 copy-start.1
  9.2 0.0 copy-start.3
  9.2 1.0 broadcast_select_fusion
  10.3 7.9 %all-to-all-start = ((bf16[32,32,384]{2,1,0:T(8,128)(2,1)}), bf16[32,32,384]{2,1,0:T(8,128)(2,1)S(1)}, u32[]{:S(2)}, u32[]{:S(2)}) async-start(bf16[32,32,384]{2,1,0:T(8,128)(2,1)} %broadcast_select_fusion), calls=%async_computation | async-start | bytes 1572864 | tf_op jit(solution)/shard_map/all_to_all | solution.py:29
  18.2 0.0 copy-done.1
  18.2 0.7 gather_fusion.2
  18.9 0.1 copy.12
  19.0 0.1 reduce-window.8
  19.0 0.1 reduce
  19.2 0.0 copy-done.3
  19.2 0.7 fusion.18
  19.9 0.7 fusion.17
  20.6 0.1 convert_reduce_fusion.1
  20.7 4.4 compare_select_fusion.2
  25.1 0.2 compare_reduce_fusion.24
  25.3 15.7 %compare_and_fusion.1 = (pred[512]{0:T(512)(128)(4,1)S(1)}, s32[512]{0:T(512)S(1)}) fusion(s32[512]{0:T(512)S(1)} %convert_reduce_fusion.1, pred[512]{0:T(512)(128)(4,1)S(1)} %get-tuple-element.33, pred[512]{0:T(512)(128)(4,1)S(1)} %get-tuple-element.31, pred[512]{0:T(512)(128)(4,1)S(1)} %get-tuple-element.32, pred[512]{0:T(512)(128)(4,1)S(1)} %get-tuple-element.30, ...), kind=kLoop, calls=%fused_computation.79 | loop fusion | flops 20992 | bytes 19556 | tf_op jit(solution)/shard_map/jit(_take)/and | solution.py:39
  41.0 18.1 %all-to-all-done = bf16[32,32,384]{2,1,0:T(8,128)(2,1)S(1)} async-done(((bf16[32,32,384]{2,1,0:T(8,128)(2,1)}), bf16[32,32,384]{2,1,0:T(8,128)(2,1)S(1)}, u32[]{:S(2)}, u32[]{:S(2)}) %all-to-all-start) | async-done | bytes 786464 | tf_op jit(solution)/shard_map/all_to_all | solution.py:29
  59.1 1.9 gather_fusion.1
  61.0 0.4 convert_reduce_fusion
  61.4 52.2 %all-reduce = (f32[512]{0:T(512)S(1)}, f32[512]{0:T(512)S(1)}) all-reduce(f32[512]{0:T(512)S(1)} %get-tuple-element.8, f32[512]{0:T(512)S(1)} %get-tuple-element.7), channel_id=1, replica_groups=mesh['dp'=32,'mp'=16] {'mp'}, use_global_device_ids=true, to_apply=%region_6.7 | all-reduce | flops 1024 | bytes 8192 | tf_op jit(solution)/shard_map/psum | solution.py:41
  113.7 0.3 fusion.12
  114.0 0.2 copy.13
  114.2 3.2 stack.2
  117.4 0.0 copy-start.2
  117.4 24.7 %all-to-all-start.1 = ((bf16[16,512,384]{1,2,0:T(8,128)(2,1)}), bf16[16,512,384]{1,2,0:T(8,128)(2,1)}, u32[]{:S(2)}, u32[]{:S(2)}) async-start(bf16[16,512,384]{1,2,0:T(8,128)(2,1)} %stack.2), calls=%async_computation.1 | async-start | bytes 12582912 | tf_op jit(solution)/shard_map/all_to_all | solution.py:13
  142.1 0.0 all-gather.2.cloned.1.call-start
  142.1 0.7 all-gather.2.cloned.1.call-update
  142.8 0.0 copy-done.2
  142.8 459.7 %all-gather.2.cloned.1.call-done = bf16[6144,768]{1,0:T(8,128)(2,1)} async-done(((bf16[192,768]{1,0:T(8,128)(2,1)}), bf16[6144,768]{1,0:T(8,128)(2,1)}) %all-gather.2.cloned.1.call-update) | async-done | bytes 9437200 | tf_op jit(solution)/shard_map/all_gather | solution.py:53
  602.5 0.0 all-to-all-done.1
  602.5 13.8 %fusion.2 = bf16[512,768]{1,0:T(8,128)(2,1)} fusion(bf16[512,6144]{0,1:T(8,128)(2,1)} %bitcast.45, bf16[6144,768]{1,0:T(8,128)(2,1)} %all-gather.2.cloned.1.call-done, f32[768]{0:T(1024)S(1)} %convert_element_type.26), kind=kOutput, calls=%fused_computation.6 | convolution fusion | flops 4857790464 | bytes 16518144 | tf_op jit(solution)/shard_map/dot_general | solution.py:52
  (14 shorter events, 0.1 us)
Async XLA Ops:
  6.5 1.9 copy-start
  9.2 8.9 %copy-start.1 = (s32[32,32]{1,0:T(8,128)S(1)}, s32[32,32]{1,0:T(8,128)}, u32[]{:S(2)}) copy-start(s32[32,32]{1,0:T(8,128)} %param.7) | copy-start | bytes 12292
  9.2 9.9 %copy-start.3 = (bf16[384]{0:T(512)(128)(2,1)S(1)}, bf16[384]{0:T(512)(128)(2,1)}, u32[]{:S(2)}) copy-start(bf16[384]{0:T(512)(128)(2,1)} %param.9) | copy-start | bytes 2308
  10.3 48.8 %all-to-all-start = ((bf16[32,32,384]{2,1,0:T(8,128)(2,1)}), bf16[32,32,384]{2,1,0:T(8,128)(2,1)S(1)}, u32[]{:S(2)}, u32[]{:S(2)}) async-start(bf16[32,32,384]{2,1,0:T(8,128)(2,1)} %broadcast_select_fusion), calls=%async_computation | async-start | bytes 1572864 | tf_op jit(solution)/shard_map/all_to_all | solution.py:29
  117.4 25.4 %copy-start.2 = (bf16[768]{0:T(1024)(128)(2,1)S(1)}, bf16[768]{0:T(1024)(128)(2,1)}, u32[]{:S(2)}) copy-start(bf16[768]{0:T(1024)(128)(2,1)} %param.11) | copy-start | bytes 4612
  117.4 485.1 %all-to-all-start.1 = ((bf16[16,512,384]{1,2,0:T(8,128)(2,1)}), bf16[16,512,384]{1,2,0:T(8,128)(2,1)}, u32[]{:S(2)}, u32[]{:S(2)}) async-start(bf16[16,512,384]{1,2,0:T(8,128)(2,1)} %stack.2), calls=%async_computation.1 | async-start | bytes 12582912 | tf_op jit(solution)/shard_map/all_to_all | solution.py:13
  142.1 460.4 %all-gather.2.cloned.1.call-start = ((), (), s32[]{:S(2)}) async-start(), calls=%async_computation.2 | async-start | bytes 9732096 | tf_op jit(solution)/shard_map/all_gather | solution.py:53
Sparse Core Ops, SparseCore 0:
  145.0 457.4 all-gather.1
